TPU v7x, 32 devices: a whole 2x2x4 slice. The times are simulated.
32 devices in a mesh: seq: 16 (over z, y, core), head: 2 (over x).
Axes of the slice: x: 2, y: 2, z: 4, core: 2. Of those that a mesh axis runs over, the one named last changes fastest.
Arguments:
- volume: bfloat16 [8192, 64], P('seq'), may hold values from -6 to 6
- vox_mask: int32 [8192, 64], P('seq'), may hold values 0 or 1
- embed: bfloat16 [64, 1024], replicated, may hold values from -0.75 to 0.75
- w_qkv: bfloat16 [3, 1024, 1024], P(None, None, 'head'), may hold values from -5 to 5
- w_out: bfloat16 [1024, 1024], P(None, 'head'), may hold values from -0.1875 to 0.1875
- w_head: bfloat16 [1024, 64], replicated, may hold values from -0.1875 to 0.1875
Outputs:
- grad_qkv: float32 [3, 1024, 1024], P(None, 'seq', 'head')
- grad_out: float32 [1024, 1024], P('seq', 'head')
All inputs are finite; a program needn't handle non-finite values. No bound on the sum of `vox_mask` on one device may be relied on, other than what follows from the above.
Results may differ from a plain program's by a relative error of at most 0.0038.
Values may be sent and summed in bfloat16 or wider, within the bound.
No kernel may reach another device: no remote copies, remote signals or barrier semaphores. Data moves between devices by JAX's collectives and lax.ppermute only.
A program may use at most 64 MiB of HBM per device.

v0:
```python
import math
import jax
import jax.numpy as jnp
from jax import lax
from jax.sharding import PartitionSpec as P

D = 1024
HEADS = 16
LEVELS = 2


def partner(shard, axis, apart):
    return lax.ppermute(shard, axis, [(i, i ^ 1 << apart) for i in range(lax.axis_size(axis))])


def head_major(rows, head_dim):
    return rows.reshape(rows.shape[0], rows.shape[1] // head_dim, head_dim).transpose(1, 0, 2)


def token_major(blocks):
    return blocks.transpose(1, 0, 2).reshape(blocks.shape[1], blocks.shape[0] * blocks.shape[2])


def softmax_rows(query_head, key_head, factor):
    scores = (
        jnp.einsum("qd,kd->qk", query_head, key_head, preferred_element_type=jnp.float32) * factor
    )
    highest = jnp.max(scores, -1, keepdims=True)
    raised = jnp.exp(scores - highest)
    return raised / jnp.sum(raised, -1, keepdims=True)


def per_device(volume, vox_mask, embed, w_qkv, w_out, w_head):
    tok_rows = volume.shape[0]
    head_dim = D // HEADS
    factor = head_dim ** (-0.5)
    seq_devices = lax.axis_size("seq")
    kept = volume * (1 - vox_mask).astype(jnp.bfloat16)
    hidden = jnp.dot(kept, embed, preferred_element_type=jnp.float32)
    normed = (hidden * lax.rsqrt(jnp.mean(hidden * hidden, -1, keepdims=True) + 1e-06)).astype(
        jnp.bfloat16
    )
    projected = jnp.einsum("td,jdc->jtc", normed, w_qkv, preferred_element_type=jnp.float32).astype(
        jnp.bfloat16
    )
    remote = [partner(projected[1:], "seq", level_bit) for level_bit in range(LEVELS)]
    key_rows = jnp.concatenate([projected[1]] + [other[0] for other in remote], 0)
    value_rows = jnp.concatenate([projected[2]] + [other[1] for other in remote], 0)
    query_heads = head_major(projected[0], head_dim)
    key_heads = head_major(key_rows, head_dim)
    value_heads = head_major(value_rows, head_dim)

    def forward_head(operands):
        query_head, key_head, value_head = operands
        weights = softmax_rows(query_head, key_head, factor).astype(jnp.bfloat16)
        return jnp.dot(weights, value_head, preferred_element_type=jnp.float32).astype(jnp.bfloat16)

    context_heads = lax.map(forward_head, (query_heads, key_heads, value_heads))
    context = token_major(context_heads)
    partial_out = jnp.einsum("tc,oc->to", context, w_out, preferred_element_type=jnp.float32)
    mixed = lax.psum(partial_out.astype(jnp.bfloat16), "head").astype(jnp.float32)
    stream = (hidden + mixed).astype(jnp.bfloat16)
    predicted = jnp.dot(stream, w_head, preferred_element_type=jnp.float32)
    loss_weight = 256.0 / math.sqrt(tok_rows * seq_devices)
    grad_pred = (
        vox_mask.astype(jnp.float32) * (predicted - volume.astype(jnp.float32)) * loss_weight
    ).astype(jnp.bfloat16)
    grad_stream = jnp.einsum(
        "tv,dv->td", grad_pred, w_head, preferred_element_type=jnp.float32
    ).astype(jnp.bfloat16)
    grad_context = jnp.dot(grad_stream, w_out, preferred_element_type=jnp.float32).astype(
        jnp.bfloat16
    )

    def backward_head(operands):
        query_head, key_head, value_head, context_head, grad_head = operands
        probs = softmax_rows(query_head, key_head, factor)
        grad_probs = jnp.einsum(
            "qd,kd->qk", grad_head, value_head, preferred_element_type=jnp.float32
        )
        offsets = jnp.sum(
            grad_head.astype(jnp.float32) * context_head.astype(jnp.float32), -1, keepdims=True
        )
        grad_scores = (probs * (grad_probs - offsets) * factor).astype(jnp.bfloat16)
        grad_query = jnp.dot(grad_scores, key_head, preferred_element_type=jnp.float32).astype(
            jnp.bfloat16
        )
        grad_key = jnp.einsum(
            "qk,qd->kd", grad_scores, query_head, preferred_element_type=jnp.float32
        ).astype(jnp.bfloat16)
        grad_value = jnp.einsum(
            "qk,qd->kd", probs.astype(jnp.bfloat16), grad_head, preferred_element_type=jnp.float32
        ).astype(jnp.bfloat16)
        return (grad_query, grad_key, grad_value)

    grad_q_heads, grad_k_heads, grad_v_heads = lax.map(
        backward_head,
        (query_heads, key_heads, value_heads, context_heads, head_major(grad_context, head_dim)),
    )
    grad_query = token_major(grad_q_heads)
    local_width = grad_query.shape[1]
    blocks_all = LEVELS + 1
    grad_keys = token_major(grad_k_heads).reshape(blocks_all, tok_rows, local_width)
    grad_values = token_major(grad_v_heads).reshape(blocks_all, tok_rows, local_width)
    returned = [
        partner(jnp.stack([grad_keys[level_bit + 1], grad_values[level_bit + 1]]), "seq", level_bit)
        for level_bit in range(LEVELS)
    ]
    own_keys = jnp.stack([grad_keys[0]] + [other[0] for other in returned])
    own_values = jnp.stack([grad_values[0]] + [other[1] for other in returned])
    source = normed
    query_term = jnp.einsum("tr,tc->rc", source, grad_query, preferred_element_type=jnp.float32)
    source = normed
    key_term = jnp.einsum("tr,jtc->rc", source, own_keys, preferred_element_type=jnp.float32)
    value_term = jnp.einsum("tr,jtc->rc", source, own_values, preferred_element_type=jnp.float32)
    key_term, value_term = (key_term, value_term)
    out_term = jnp.einsum("tr,tc->rc", grad_stream, context, preferred_element_type=jnp.float32)
    summed = lax.psum_scatter(
        jnp.stack([query_term, key_term, value_term, out_term], 1),
        "seq",
        scatter_dimension=0,
        tiled=True,
    )
    return (jnp.transpose(summed[:, :3, :], (1, 0, 2)), summed[:, 3, :])


def solution(mesh):
    return jax.shard_map(
        per_device,
        mesh=mesh,
        in_specs=(P("seq", None), P("seq", None), P(), P(None, None, "head"), P(None, "head"), P()),
        out_specs=(P(None, "seq", "head"), P("seq", "head")),
        check_vma=False,
    )
```

profile of v0, /device:TPU:0, one launch (start us, length us, event | category | flops | bytes accessed | tf_op | source)
XLA Modules:
  0.0 395.8 jit_solution(14222275033119210577)
XLA Ops:
  10.5 1.8 fusion.46
  13.9 2.5 collective-permute-start.1
  18.8 2.2 fusion.67
  22.6 17.9 %collective-permute-done.1 = bf16[2,512,512]{1,2,0:T(8,128)(2,1)} collective-permute-done((bf16[2,512,512]{1,2,0:T(8,128)(2,1)}, bf16[2,512,512]{1,2,0:T(8,128)(2,1)}, u32[]{:S(2)}, u32[]{:S(2)}) %collective-permute-start.1) | collective-permute-done | bytes 1048608 | tf_op jit(solution)/shard_map/ppermute | solution.py:13
  40.5 2.3 fusion.68
  42.8 2.4 copy.22
  45.2 2.3 copy.24
  47.5 2.4 copy.25
  49.9 4.6 %maximum_bitcast_fusion = (bf16[8,1536,64]{2,1,0:T(8,128)(2,1)}, bf16[8,1536,64]{2,1,0:T(8,128)(2,1)}) fusion(bf16[512,8,64]{2,0,1:T(8,128)(2,1)} %copy.22, bf16[512,8,64]{2,0,1:T(8,128)(2,1)S(1)} %copy.21, bf16[512,8,64]{2,0,1:T(8,128)(2,1)S(1)} %copy.20, bf16[512,8,64]{2,0,1:T(8,128)(2,1)} %copy.25, bf16[512,8,64]{2,0,1:T(8,128)(2,1)} %copy.24, ...), kind=kLoop, calls=%fused_computation.57 | loop fusion | flops 9437184 | bytes 6291456 | tf_op jit(solution)/shard_map/transpose | solution.py:17
  55.3 37.6 %while.24 = (s32[]{:T(128)}, bf16[8,512,64]{1,2,0:T(8,128)(2,1)}, bf16[8,512,64]{2,1,0:T(8,128)(2,1)}, bf16[8,1536,64]{2,1,0:T(8,128)(2,1)}, bf16[8,1536,64]{2,1,0:T(8,128)(2,1)}, /*index=5*/s32[]{:T(128)}) while((s32[]{:T(128)}, bf16[8,512,64]{1,2,0:T(8,128)(2,1)}, bf16[8,512,64]{2,1,0:T(8,128)(2,1)}, bf16[8,1536,64]{2,1,0:T(8,128)(2,1)}, ...), condition=%wide.region_4.5_spmd, body=%wide.region_1.4_spmd.sunk | while | flops 206863360 | bytes 10432581 | solution.py:58
  55.3 1.7 fusion.107
  57.6 2.4 fusion.109
  62.3 2.4 fusion.109
  67.0 2.4 fusion.109
  71.7 2.4 fusion.109
  74.1 1.7 fusion.107
  76.4 2.4 fusion.109
  81.1 2.4 fusion.109
  85.8 2.4 fusion.109
  90.5 2.4 fusion.109
  92.9 3.3 convolution_convert_fusion.5
  96.5 41.5 %all-reduce.2.cloned.1.call-done = bf16[512,1024]{1,0:T(8,128)(2,1)} async-done(((bf16[512,1024]{1,0:T(8,128)(2,1)}), bf16[512,1024]{1,0:T(8,128)(2,1)}) %all-reduce.2.cloned.1.call-update) | async-done | bytes 1048592 | tf_op jit(solution)/shard_map/psum | solution.py:61
  138.0 2.1 convolution_convert_fusion.4
  140.1 2.4 convolution_convert_fusion.6
  144.7 103.3 %while.25 = (s32[]{:T(128)}, bf16[8,512,64]{1,2,0:T(8,128)(2,1)}, bf16[8,1536,64]{1,2,0:T(8,128)(2,1)}, bf16[8,1536,64]{1,2,0:T(8,128)(2,1)}, bf16[8,512,64]{2,1...) while((s32[]{:T(128)}, bf16[8,512,64]{1,2,0:T(8,128)(2,1)}, ...), condition=%wide.region_10.11_spmd, body=%wide.region_6.10_spmd.sunk | while | flops 513899008 | bytes 19881068 | solution.py:96
  144.7 1.7 fusion.119
  147.0 2.3 fusion.124
  151.4 2.0 fusion.121
  153.4 2.0 fusion.123
  155.4 2.2 fusion.122
  159.9 2.3 fusion.124
  164.3 2.0 fusion.121
  166.3 2.0 fusion.123
  168.3 2.2 fusion.122
  172.8 2.3 fusion.124
  177.2 2.0 fusion.121
  179.2 2.0 fusion.123
  181.2 2.2 fusion.122
  185.7 2.3 fusion.124
  190.1 2.0 fusion.121
  192.1 2.0 fusion.123
  194.1 2.2 fusion.122
  198.6 2.3 fusion.124
  203.0 2.0 fusion.121
  205.0 2.0 fusion.123
  207.1 2.2 fusion.122
  211.6 2.3 fusion.124
  215.9 2.0 fusion.121
  217.9 2.0 fusion.123
  220.0 2.2 fusion.122
  224.5 2.3 fusion.124
  228.8 2.0 fusion.121
  230.9 2.0 fusion.123
  232.9 2.2 fusion.122
  237.4 2.3 fusion.124
  241.7 2.0 fusion.121
  243.8 2.0 fusion.123
  245.8 2.2 fusion.122
  251.8 1.8 convolution_bitcast_fusion
  253.7 1.8 convolution_bitcast_fusion.1
  255.5 20.4 %collective-permute-done.3 = bf16[2,512,512]{1,2,0:T(8,128)(2,1)S(1)} collective-permute-done((bf16[2,512,512]{1,2,0:T(8,128)(2,1)S(1)}, bf16[2,512,512]{1,2,0:T(8,128)(2,1)S(1)}, u32[]{:S(2)}, u32[]{:S(2)}) %collective-permute-start.3) | collective-permute-done | bytes 1048608 | tf_op jit(solution)/shard_map/ppermute | solution.py:13
  278.0 4.0 pad_maximum_fusion
  282.0 103.6 %reduce-scatter.2.cloned.1.call-done = f32[64,4,512]{2,0,1:T(8,128)} async-done(((f32[1024,4,512]{2,0,1:T(8,128)}), f32[64,4,512]{2,0,1:T(8,128)}) %reduce-scatter.2.cloned.1.call-update) | async-done | bytes 524304 | tf_op jit(solution)/shard_map/reduce_scatter | solution.py:118
  385.6 1.8 slice_bitcast_fusion
  (111 shorter events, 67.2 us)
Async XLA Ops:
  7.2 3.3 copy-start
  7.2 130.8 %all-reduce.2.cloned.1.call-start = ((), (), s32[]{:S(2)}) async-start(), calls=%async_computation.1 | async-start | bytes 2097152 | tf_op jit(solution)/shard_map/psum | solution.py:61
  8.9 1.4 copy-start.2
  10.5 1.9 copy-start.4
  13.4 5.4 %collective-permute-start = (bf16[2,512,512]{1,2,0:T(8,128)(2,1)}, bf16[2,512,512]{1,2,0:T(8,128)(2,1)}, u32[]{:S(2)}, u32[]{:S(2)}) collective-permute-start(bf16[2,512,512]{1,2,0:T(8,128)(2,1)} %slice.107), channel_id=1, source_target_pairs={{0,2},{2,0},{4,6},{6,4},{8,10},{10,8},{12,14},{14,12},{16,18},{18,... | collective-permute-start | bytes 3145736 | tf_op jit(solution)/shard_map/ppermute | solution.py:13
  13.9 26.6 %collective-permute-start.1 = (bf16[2,512,512]{1,2,0:T(8,128)(2,1)}, bf16[2,512,512]{1,2,0:T(8,128)(2,1)}, u32[]{:S(2)}, u32[]{:S(2)}) collective-permute-start(bf16[2,512,512]{1,2,0:T(8,128)(2,1)} %slice.107), channel_id=1, source_target_pairs={{0,4},{2,6},{4,0},{6,2},{8,12},{10,14},{12,8},{14,10},{16,20},{18,... | collective-permute-start | bytes 3145736 | tf_op jit(solution)/shard_map/ppermute | solution.py:13
  92.9 45.1 %copy-start.3 = (f32[512,1024]{1,0:T(8,128)S(1)}, f32[512,1024]{1,0:T(8,128)}, u32[]{:S(2)}) copy-start(f32[512,1024]{1,0:T(8,128)} %copy-done.2) | copy-start | bytes 6291460
  92.9 45.1 %copy-start.9 = (s32[512,64]{0,1:T(8,128)S(1)}, s32[512,64]{0,1:T(8,128)}, u32[]{:S(2)}) copy-start(s32[512,64]{0,1:T(8,128)} %param.11) | copy-start | bytes 393220
  92.9 45.1 %copy-start.10 = (bf16[1024,64]{0,1:T(8,128)(2,1)S(1)}, bf16[1024,64]{0,1:T(8,128)(2,1)}, u32[]{:S(2)}) copy-start(bf16[1024,64]{0,1:T(8,128)(2,1)} %param.15) | copy-start | bytes 393220
  92.9 45.1 %copy-start.11 = (bf16[512,64]{0,1:T(8,128)(2,1)S(1)}, bf16[512,64]{0,1:T(8,128)(2,1)}, u32[]{:S(2)}) copy-start(bf16[512,64]{0,1:T(8,128)(2,1)} %param.10) | copy-start | bytes 196612
  96.3 289.3 %reduce-scatter.2.cloned.1.call-start = ((), (), s32[]{:S(2)}) async-start(), calls=%async_computation.2 | async-start | bytes 8912896 | tf_op jit(solution)/shard_map/reduce_scatter | solution.py:118
  140.1 4.6 %copy-start.6 = (bf16[512,1024]{1,0:T(8,128)(2,1)}, bf16[512,1024]{1,0:T(8,128)(2,1)S(1)}, u32[]{:S(2)}) copy-start(bf16[512,1024]{1,0:T(8,128)(2,1)S(1)} %convolution_convert_fusion.4) | copy-start | bytes 3145732
  248.0 1.9 copy-start.8
  249.9 2.0 copy-start.7
  250.1 3.6 copy-start.5
  250.1 5.4 %collective-permute-start.2 = (bf16[2,512,512]{1,2,0:T(8,128)(2,1)S(1)}, bf16[2,512,512]{1,2,0:T(8,128)(2,1)S(1)}, u32[]{:S(2)}, u32[]{:S(2)}) collective-permute-start(bf16[2,512,512]{1,2,0:T(8,128)(2,1)S(1)} %pad_maximum_fusion.1), channel_id=1, source_target_pairs={{0,2},{2,0},{4,6},{6,4},{8,10},{10,8},{12,14},{14,12},{16,18},{18,... | collective-permute-start | bytes 3145736 | tf_op jit(solution)/shard_map/ppermute | solution.py:13
  250.3 25.6 %collective-permute-start.3 = (bf16[2,512,512]{1,2,0:T(8,128)(2,1)S(1)}, bf16[2,512,512]{1,2,0:T(8,128)(2,1)S(1)}, u32[]{:S(2)}, u32[]{:S(2)}) collective-permute-start(bf16[2,512,512]{1,2,0:T(8,128)(2,1)S(1)} %pad_maximum_fusion.2), channel_id=1, source_target_pairs={{0,4},{2,6},{4,0},{6,2},{8,12},{10,14},{12,8},{14,10},{16,20},{18,... | collective-permute-start | bytes 3145736 | tf_op jit(solution)/shard_map/ppermute | solution.py:13
  282.0 107.0 %copy-start.1 = (bf16[3,1024,512]{2,1,0:T(8,128)(2,1)S(1)}, bf16[3,1024,512]{2,1,0:T(8,128)(2,1)}, u32[]{:S(2)}) copy-start(bf16[3,1024,512]{2,1,0:T(8,128)(2,1)} %param.13) | copy-start | bytes 9437188
Sparse Core Ops, SparseCore 0:
  96.4 41.5 all-reduce.1
  282.1 103.4 reduce-scatter.1
where the time goes:
time: 398 us; the launch traced here: 396 us
  waiting for transfers between devices  183 us (46%)
  matrix products  132 us (33%)
  local copies, waits for them, and re-layouts  34.2 us (9%)
  other arithmetic  27 us (7%)
  between operations  14.3 us (4%)
  starting transfers between devices  4.87 us (1%)
    reduce_scatter x1, waiting for transfers between devices, per_device(): lax.psum_scatter(jnp.stack([query_term, key_term, value_term, out_term],...  104 us
    psum x1, waiting for transfers between devices, per_device(): lax.psum(partial_out.astype(jnp.bfloat16), 'head').astype(jnp.float32)  41.5 us
    ppermute x4, waiting for transfers between devices, partner(): lax.ppermute(shard, axis, [(i, i ^ 1 << apart) for i in range(lax.axis_si...  38.3 us
    dot_general x16, matrix products, softmax_rows(): jnp.einsum('qd,kd->qk', query_head, key_head, preferred_element_type=jnp....  27.6 us
    dot_general x8, matrix products, forward_head(): jnp.dot(weights, value_head, preferred_element_type=jnp.float32)  19.2 us
    dot_general x8, matrix products, backward_head(): jnp.einsum('qk,qd->kd', probs.astype(jnp.bfloat16), grad_head, preferred_...  18.7 us
    dot_general x8, matrix products, backward_head(): jnp.dot(grad_scores, key_head, preferred_element_type=jnp.float32)  17.7 us
    dot_general x8, matrix products, backward_head(): jnp.einsum('qk,qd->kd', grad_scores, query_head, preferred_element_type=j...  16.2 us
  transfers between devices with their start and end apart: 6, of which 4 were waited for; matrix products, arithmetic and copies ran while one was open for 3% of the time, Pallas kernels for 0%

commit v1 on v0

--- a/solution.py
+++ b/solution.py
@@ -58,7 +58,9 @@
     context_heads = lax.map(forward_head, (query_heads, key_heads, value_heads))
     context = token_major(context_heads)
     partial_out = jnp.einsum("tc,oc->to", context, w_out, preferred_element_type=jnp.float32)
-    mixed = lax.psum(partial_out.astype(jnp.bfloat16), "head").astype(jnp.float32)
+    mixed = jnp.sum(lax.all_gather(partial_out.astype(jnp.bfloat16), "head"), axis=0).astype(
+        jnp.float32
+    )
     stream = (hidden + mixed).astype(jnp.bfloat16)
     predicted = jnp.dot(stream, w_head, preferred_element_type=jnp.float32)
     loss_weight = 256.0 / math.sqrt(tok_rows * seq_devices)

time: 398 us -> 395 us (level)
  waiting for transfers between devices: 183 us -> 176 us
    psum x1 -> x0, waiting for transfers between devices: 41.5 us -> none  [per_device(): lax.psum(partial_out.astype(jnp.bfloat16), 'head').astype(jnp.float32)]
    all_gather x0 -> x1, waiting for transfers between devices: none -> 34.5 us  [per_device(): lax.all_gather(partial_out.astype(jnp.bfloat16), 'head')]
where the time goes in v1:
time: 395 us; the launch traced here: 392 us
  waiting for transfers between devices  176 us (45%)
  matrix products  132 us (33%)
  local copies, waits for them, and re-layouts  34.2 us (9%)
  other arithmetic  30.3 us (8%)
  between operations  14.3 us (4%)
  starting transfers between devices  4.87 us (1%)
    reduce_scatter x1, waiting for transfers between devices, per_device(): lax.psum_scatter(jnp.stack([query_term, key_term, value_term, out_term],...  104 us
    ppermute x4, waiting for transfers between devices, partner(): lax.ppermute(shard, axis, [(i, i ^ 1 << apart) for i in range(lax.axis_si...  38.3 us
    all_gather x1, waiting for transfers between devices, per_device(): lax.all_gather(partial_out.astype(jnp.bfloat16), 'head')  34.5 us
    dot_general x16, matrix products, softmax_rows(): jnp.einsum('qd,kd->qk', query_head, key_head, preferred_element_type=jnp....  27.6 us
    dot_general x8, matrix products, forward_head(): jnp.dot(weights, value_head, preferred_element_type=jnp.float32)  19.3 us
    dot_general x8, matrix products, backward_head(): jnp.einsum('qk,qd->kd', probs.astype(jnp.bfloat16), grad_head, preferred_...  18.8 us
    dot_general x8, matrix products, backward_head(): jnp.dot(grad_scores, key_head, preferred_element_type=jnp.float32)  17.7 us
    dot_general x8, matrix products, backward_head(): jnp.einsum('qk,qd->kd', grad_scores, query_head, preferred_element_type=j...  16.1 us
  transfers between devices with their start and end apart: 6, of which 4 were waited for; matrix products, arithmetic and copies ran while one was open for 3% of the time, Pallas kernels for 0%

profile of v1, /device:TPU:0, one launch (start us, length us, event | category | flops | bytes accessed | tf_op | source)
XLA Modules:
  0.0 392.2 jit_solution(2212269871810560026)
XLA Ops:
  10.5 1.8 fusion.46
  13.9 2.5 collective-permute-start.1
  18.8 2.3 fusion.67
  22.6 17.9 %collective-permute-done.1 = bf16[2,512,512]{1,2,0:T(8,128)(2,1)} collective-permute-done((bf16[2,512,512]{1,2,0:T(8,128)(2,1)}, bf16[2,512,512]{1,2,0:T(8,128)(2,1)}, u32[]{:S(2)}, u32[]{:S(2)}) %collective-permute-start.1) | collective-permute-done | bytes 1048608 | tf_op jit(solution)/shard_map/ppermute | solution.py:13
  40.5 2.3 fusion.68
  42.8 2.4 copy.22
  45.2 2.3 copy.24
  47.6 2.4 copy.25
  49.9 4.6 %maximum_bitcast_fusion = (bf16[8,1536,64]{2,1,0:T(8,128)(2,1)}, bf16[8,1536,64]{2,1,0:T(8,128)(2,1)}) fusion(bf16[512,8,64]{2,0,1:T(8,128)(2,1)} %copy.22, bf16[512,8,64]{2,0,1:T(8,128)(2,1)S(1)} %copy.21, bf16[512,8,64]{2,0,1:T(8,128)(2,1)S(1)} %copy.20, bf16[512,8,64]{2,0,1:T(8,128)(2,1)} %copy.25, bf16[512,8,64]{2,0,1:T(8,128)(2,1)} %copy.24, ...), kind=kLoop, calls=%fused_computation.57 | loop fusion | flops 9437184 | bytes 6291456 | tf_op jit(solution)/shard_map/transpose | solution.py:17
  55.4 37.6 %while.24 = (s32[]{:T(128)}, bf16[8,512,64]{1,2,0:T(8,128)(2,1)}, bf16[8,512,64]{2,1,0:T(8,128)(2,1)}, bf16[8,1536,64]{2,1,0:T(8,128)(2,1)}, bf16[8,1536,64]{2,1,0:T(8,128)(2,1)}, /*index=5*/s32[]{:T(128)}) while((s32[]{:T(128)}, bf16[8,512,64]{1,2,0:T(8,128)(2,1)}, bf16[8,512,64]{2,1,0:T(8,128)(2,1)}, bf16[8,1536,64]{2,1,0:T(8,128)(2,1)}, ...), condition=%wide.region_4.5_spmd, body=%wide.region_1.4_spmd.sunk | while | flops 206863360 | bytes 10432581 | solution.py:58
  57.7 2.4 fusion.109
  62.4 2.4 fusion.109
  67.1 2.4 fusion.109
  71.8 2.4 fusion.109
  76.5 2.4 fusion.109
  81.2 2.4 fusion.109
  85.9 2.4 fusion.109
  90.6 2.4 fusion.109
  93.0 3.3 convolution_convert_fusion.5
  96.6 34.5 %all-gather.3.cloned.1.call-done = bf16[1024,1024]{1,0:T(8,128)(2,1)} async-done(((bf16[512,1024]{1,0:T(8,128)(2,1)}), bf16[1024,1024]{1,0:T(8,128)(2,1)}) %all-gather.3.cloned.1.call-update) | async-done | bytes 2097168 | tf_op jit(solution)/shard_map/all_gather | solution.py:61
  131.0 3.3 reduce_sum.67
  134.4 2.1 convolution_convert_fusion.4
  136.5 2.4 convolution_convert_fusion.6
  141.1 103.3 %while.25 = (s32[]{:T(128)}, bf16[8,512,64]{1,2,0:T(8,128)(2,1)}, bf16[8,1536,64]{1,2,0:T(8,128)(2,1)}, bf16[8,1536,64]{1,2,0:T(8,128)(2,1)}, bf16[8,512,64]{2,1...) while((s32[]{:T(128)}, bf16[8,512,64]{1,2,0:T(8,128)(2,1)}, ...), condition=%wide.region_10.11_spmd, body=%wide.region_6.10_spmd.sunk | while | flops 513899008 | bytes 19881068 | solution.py:98
  143.4 2.3 fusion.124
  147.8 2.0 fusion.121
  149.8 2.0 fusion.123
  151.8 2.2 fusion.122
  154.0 1.7 fusion.119
  156.3 2.3 fusion.124
  160.7 2.0 fusion.121
  162.7 2.0 fusion.123
  164.7 2.2 fusion.122
  166.9 1.7 fusion.119
  169.2 2.3 fusion.124
  173.6 2.0 fusion.121
  175.6 2.0 fusion.123
  177.7 2.2 fusion.122
  182.2 2.3 fusion.124
  186.5 2.0 fusion.121
  188.5 2.0 fusion.123
  190.6 2.2 fusion.122
  195.1 2.4 fusion.124
  199.5 2.0 fusion.121
  201.5 2.0 fusion.123
  203.5 2.2 fusion.122
  208.0 2.3 fusion.124
  212.4 2.0 fusion.121
  214.4 2.0 fusion.123
  216.4 2.2 fusion.122
  220.9 2.4 fusion.124
  225.3 2.0 fusion.121
  227.3 2.0 fusion.123
  229.3 2.2 fusion.122
  233.8 2.3 fusion.124
  238.2 2.0 fusion.121
  240.2 2.0 fusion.123
  242.2 2.2 fusion.122
  248.2 1.8 convolution_bitcast_fusion
  250.1 1.8 convolution_bitcast_fusion.1
  252.0 20.4 %collective-permute-done.3 = bf16[2,512,512]{1,2,0:T(8,128)(2,1)S(1)} collective-permute-done((bf16[2,512,512]{1,2,0:T(8,128)(2,1)S(1)}, bf16[2,512,512]{1,2,0:T(8,128)(2,1)S(1)}, u32[]{:S(2)}, u32[]{:S(2)}) %collective-permute-start.3) | collective-permute-done | bytes 1048608 | tf_op jit(solution)/shard_map/ppermute | solution.py:13
  274.4 4.0 %pad_maximum_fusion = f32[1024,4,512]{2,0,1:T(8,128)} fusion(f32[1024,1,512]{2,0,1:T(8,128)S(1)} %convolution_bitcast_fusion, f32[1024,1,512]{2,0,1:T(8,128)S(1)} %convolution_bitcast_fusion.2, f32[1024,1,512]{2,0,1:T(8,128)S(1)} %convolution_bitcast_fusion.3, f32[1024,1,512]{2,0,1:T(8,128)S(1)} %convolution_bitcast_fusion.1), kind=kLoop, calls=%fused_computation.56 | loop fusion | flops 6291456 | bytes 16777216 | tf_op jit(solution)/shard_map/stack | solution.py:121
  278.4 103.6 %reduce-scatter.2.cloned.1.call-done = f32[64,4,512]{2,0,1:T(8,128)} async-done(((f32[1024,4,512]{2,0,1:T(8,128)}), f32[64,4,512]{2,0,1:T(8,128)}) %reduce-scatter.2.cloned.1.call-update) | async-done | bytes 524304 | tf_op jit(solution)/shard_map/reduce_scatter | solution.py:120
  382.0 1.8 slice_bitcast_fusion
  (112 shorter events, 69.0 us)
Async XLA Ops:
  7.2 3.3 copy-start
  7.2 123.9 %all-gather.3.cloned.1.call-start = ((), (), s32[]{:S(2)}) async-start(), calls=%async_computation.2 | async-start | bytes 3145728 | tf_op jit(solution)/shard_map/all_gather | solution.py:61
  8.9 1.4 copy-start.2
  10.5 1.9 copy-start.4
  13.4 5.4 %collective-permute-start = (bf16[2,512,512]{1,2,0:T(8,128)(2,1)}, bf16[2,512,512]{1,2,0:T(8,128)(2,1)}, u32[]{:S(2)}, u32[]{:S(2)}) collective-permute-start(bf16[2,512,512]{1,2,0:T(8,128)(2,1)} %slice.107), channel_id=1, source_target_pairs={{0,2},{2,0},{4,6},{6,4},{8,10},{10,8},{12,14},{14,12},{16,18},{18,... | collective-permute-start | bytes 3145736 | tf_op jit(solution)/shard_map/ppermute | solution.py:13
  13.9 26.6 %collective-permute-start.1 = (bf16[2,512,512]{1,2,0:T(8,128)(2,1)}, bf16[2,512,512]{1,2,0:T(8,128)(2,1)}, u32[]{:S(2)}, u32[]{:S(2)}) collective-permute-start(bf16[2,512,512]{1,2,0:T(8,128)(2,1)} %slice.107), channel_id=1, source_target_pairs={{0,4},{2,6},{4,0},{6,2},{8,12},{10,14},{12,8},{14,10},{16,20},{18,... | collective-permute-start | bytes 3145736 | tf_op jit(solution)/shard_map/ppermute | solution.py:13
  93.0 41.4 %copy-start.3 = (f32[512,1024]{1,0:T(8,128)S(1)}, f32[512,1024]{1,0:T(8,128)}, u32[]{:S(2)}) copy-start(f32[512,1024]{1,0:T(8,128)} %copy-done.2) | copy-start | bytes 6291460
  93.0 41.4 %copy-start.9 = (s32[512,64]{0,1:T(8,128)S(1)}, s32[512,64]{0,1:T(8,128)}, u32[]{:S(2)}) copy-start(s32[512,64]{0,1:T(8,128)} %param.11) | copy-start | bytes 393220
  93.0 41.4 %copy-start.10 = (bf16[1024,64]{0,1:T(8,128)(2,1)S(1)}, bf16[1024,64]{0,1:T(8,128)(2,1)}, u32[]{:S(2)}) copy-start(bf16[1024,64]{0,1:T(8,128)(2,1)} %param.15) | copy-start | bytes 393220
  93.0 41.4 %copy-start.11 = (bf16[512,64]{0,1:T(8,128)(2,1)S(1)}, bf16[512,64]{0,1:T(8,128)(2,1)}, u32[]{:S(2)}) copy-start(bf16[512,64]{0,1:T(8,128)(2,1)} %param.10) | copy-start | bytes 196612
  96.3 285.7 %reduce-scatter.2.cloned.1.call-start = ((), (), s32[]{:S(2)}) async-start(), calls=%async_computation.1 | async-start | bytes 8912896 | tf_op jit(solution)/shard_map/reduce_scatter | solution.py:120
  136.5 4.6 %copy-start.6 = (bf16[512,1024]{1,0:T(8,128)(2,1)}, bf16[512,1024]{1,0:T(8,128)(2,1)S(1)}, u32[]{:S(2)}) copy-start(bf16[512,1024]{1,0:T(8,128)(2,1)S(1)} %convolution_convert_fusion.4) | copy-start | bytes 3145732
  244.4 1.9 copy-start.8
  246.3 2.0 copy-start.7
  246.5 3.5 copy-start.5
  246.5 5.4 %collective-permute-start.2 = (bf16[2,512,512]{1,2,0:T(8,128)(2,1)S(1)}, bf16[2,512,512]{1,2,0:T(8,128)(2,1)S(1)}, u32[]{:S(2)}, u32[]{:S(2)}) collective-permute-start(bf16[2,512,512]{1,2,0:T(8,128)(2,1)S(1)} %pad_maximum_fusion.1), channel_id=1, source_target_pairs={{0,2},{2,0},{4,6},{6,4},{8,10},{10,8},{12,14},{14,12},{16,18},{18,... | collective-permute-start | bytes 3145736 | tf_op jit(solution)/shard_map/ppermute | solution.py:13
  246.7 25.6 %collective-permute-start.3 = (bf16[2,512,512]{1,2,0:T(8,128)(2,1)S(1)}, bf16[2,512,512]{1,2,0:T(8,128)(2,1)S(1)}, u32[]{:S(2)}, u32[]{:S(2)}) collective-permute-start(bf16[2,512,512]{1,2,0:T(8,128)(2,1)S(1)} %pad_maximum_fusion.2), channel_id=1, source_target_pairs={{0,4},{2,6},{4,0},{6,2},{8,12},{10,14},{12,8},{14,10},{16,20},{18,... | collective-permute-start | bytes 3145736 | tf_op jit(solution)/shard_map/ppermute | solution.py:13
  278.4 107.0 %copy-start.1 = (bf16[3,1024,512]{2,1,0:T(8,128)(2,1)S(1)}, bf16[3,1024,512]{2,1,0:T(8,128)(2,1)}, u32[]{:S(2)}) copy-start(bf16[3,1024,512]{2,1,0:T(8,128)(2,1)} %param.13) | copy-start | bytes 9437188
Sparse Core Ops, SparseCore 0:
  96.4 34.5 all-gather.2
  278.5 103.4 reduce-scatter.1
